TPU v7x, 512 devices: a whole 4x8x8 slice. The times are simulated.
512 devices in a mesh: ctx: 32 (over z, x), head: 16 (over y, core).
Axes of the slice: x: 4, y: 8, z: 8, core: 2. Of those that a mesh axis runs over, the one named last changes fastest.
Arguments:
- queries: bfloat16 [16384, 4096], P(('ctx', 'head')), may hold values from -64 to 64
- keys: bfloat16 [16384, 4096], P(('ctx', 'head')), may hold values from -8 to 8
- values: bfloat16 [16384, 4096], P(('ctx', 'head')), may hold values from -6 to 6
Outputs:
- attended: bfloat16 [16384, 4096], P(('ctx', 'head'))
All inputs are finite; a program needn't handle non-finite values.
Results may differ from a plain program's by a relative error of at most 0.0045.
Values may be sent and summed in bfloat16 or wider, within the bound.
No kernel may reach another device: no remote copies, remote signals or barrier semaphores. Data moves between devices by JAX's collectives and lax.ppermute only.
A program may use at most 64 MiB of HBM per device.

v0:
```python
import jax
import jax.numpy as jnp
from jax import lax
from jax.sharding import PartitionSpec as P

HEAD_SIZE = 128
BLOCK = 256
SUM = 16
BAND_REACH = 1024


def from_behind(value, axis, steps):
    count = lax.axis_size(axis)
    initial, last = (max(0, -steps), min(count, count - steps))
    return lax.ppermute(value, axis, [(source, source + steps) for source in range(initial, last)])


def summary_positions(count):
    ridx = jnp.arange(count, dtype=jnp.int32)
    return ridx // SUM * BLOCK + BLOCK - SUM + ridx % SUM


def band_scores(qblk, kb, qpos, bpos):
    scores = jnp.einsum(
        "qhd,khd->hqk", qblk, kb, preferred_element_type=jnp.float32
    ) * HEAD_SIZE ** (-0.5)
    diff = qpos[:, None] - bpos[None, :]
    band_ok = (bpos[None, :] >= 0) & (diff >= 0) & (diff < BAND_REACH)
    return (jnp.where(band_ok[None], scores, -1e30), band_ok)


def sum_scores(qblk, ks, qpos, spos):
    scores = jnp.einsum(
        "qhd,khd->hqk", qblk, ks, preferred_element_type=jnp.float32
    ) * HEAD_SIZE ** (-0.5)
    sum_ok = qpos[:, None] - spos[None, :] >= BAND_REACH
    return (jnp.where(sum_ok[None], scores, -1e30), sum_ok)


def local(queries, keys, values):
    q_dev, k_dev, v_dev = (
        lax.all_to_all(queries, "head", split_axis=1, concat_axis=0, tiled=True),
        lax.all_to_all(keys, "head", split_axis=1, concat_axis=0, tiled=True),
        lax.all_to_all(values, "head", split_axis=1, concat_axis=0, tiled=True),
    )
    tok_rows = q_dev.shape[0]
    heads_here = q_dev.shape[1] // HEAD_SIZE
    q_all = q_dev.reshape(tok_rows, heads_here, HEAD_SIZE)
    k_all = k_dev.reshape(tok_rows, heads_here, HEAD_SIZE)
    value_rows_all = v_dev.reshape(tok_rows, heads_here, HEAD_SIZE)
    base = lax.axis_index("ctx") * tok_rows
    reach_devs = (BAND_REACH + tok_rows - 1) // tok_rows
    band_k_parts = []
    band_v_parts = []
    for dist in range(reach_devs, 0, -1):
        prev_k, prev_v = from_behind((k_all, value_rows_all), "ctx", dist)
        band_k_parts.append(prev_k)
        band_v_parts.append(prev_v)
    k_band = jnp.concatenate(band_k_parts + [k_all], axis=0)
    v_band = jnp.concatenate(band_v_parts + [value_rows_all], axis=0)
    k_sum = k_all.reshape(tok_rows // BLOCK, BLOCK, heads_here, HEAD_SIZE)[
        :, BLOCK - SUM :
    ].reshape(-1, heads_here, HEAD_SIZE)
    v_sum = value_rows_all.reshape(tok_rows // BLOCK, BLOCK, heads_here, HEAD_SIZE)[
        :, BLOCK - SUM :
    ].reshape(-1, heads_here, HEAD_SIZE)
    query_rows = min(512, tok_rows)
    k_seen, v_seen = (
        lax.all_gather(k_sum, "ctx", axis=0, tiled=True),
        lax.all_gather(v_sum, "ctx", axis=0, tiled=True),
    )
    spos = summary_positions(k_seen.shape[0])
    qpos = base + 0 + jnp.arange(query_rows, dtype=jnp.int32)
    bpos = base + 0 - BAND_REACH + jnp.arange(BAND_REACH + query_rows, dtype=jnp.int32)
    sb, band_ok = band_scores(q_all, k_band, qpos, bpos)
    ss, sum_ok = sum_scores(q_all, k_seen, qpos, spos)
    top = jnp.maximum(jnp.max(sb, axis=-1), jnp.max(ss, axis=-1))
    pb = jnp.where(band_ok[None], jnp.exp(sb - top[..., None]), 0.0)
    ps = jnp.where(sum_ok[None], jnp.exp(ss - top[..., None]), 0.0)
    total = jnp.sum(pb, axis=-1) + jnp.sum(ps, axis=-1)
    numer = jnp.einsum(
        "hqk,khd->hqd", pb.astype(jnp.bfloat16), v_band, preferred_element_type=jnp.float32
    )
    numer = numer + jnp.einsum(
        "hqk,khd->hqd", ps.astype(jnp.bfloat16), v_seen, preferred_element_type=jnp.float32
    )
    outputs = (numer / total[..., None]).astype(jnp.bfloat16)
    local_out = jnp.transpose(outputs, (1, 0, 2)).reshape(tok_rows, heads_here * HEAD_SIZE)
    return lax.all_to_all(local_out, "head", split_axis=0, concat_axis=1, tiled=True)


def solution(mesh):
    placed = (P(("ctx", "head"), None), P(("ctx", "head"), None), P(("ctx", "head"), None))
    return jax.shard_map(
        local, mesh=mesh, in_specs=placed, out_specs=P(("ctx", "head"), None), check_vma=False
    )
```

profile of v0, /device:TPU:1, one launch (start us, length us, event | category | flops | bytes accessed | tf_op | source)
XLA Modules:
  0.0 202.9 jit_solution(5113818668140750158)
XLA Ops:
  0.0 1.7 copy.54
  1.7 10.2 %all-to-all-start = ((bf16[32,16,256]{2,0,1:T(8,128)(2,1)}), bf16[32,16,256]{2,0,1:T(8,128)(2,1)S(1)}, u32[]{:S(2)}, u32[]{:S(2)}) async-start(bf16[32,16,256]{2,0,1:T(8,128)(2,1)} %bitcast.48), calls=%async_computation | async-start | bytes 524288 | tf_op jit(solution)/shard_map/all_to_all | solution.py:43
  11.9 1.7 copy.52
  13.5 10.2 %all-to-all-done = bf16[32,16,256]{2,0,1:T(8,128)(2,1)S(1)} async-done(((bf16[32,16,256]{2,0,1:T(8,128)(2,1)}), bf16[32,16,256]{2,0,1:T(8,128)(2,1)S(1)}, u32[]{:S(2)}, u32[]{:S(2)}) %all-to-all-start) | async-done | bytes 262176 | tf_op jit(solution)/shard_map/all_to_all | solution.py:43
  23.7 3.4 %all-to-all-start.2 = ((bf16[32,16,256]{2,0,1:T(8,128)(2,1)}), bf16[32,16,256]{2,0,1:T(8,128)(2,1)S(1)}, u32[]{:S(2)}, u32[]{:S(2)}) async-start(bf16[32,16,256]{2,0,1:T(8,128)(2,1)} %bitcast.46), calls=%async_computation.2 | async-start | bytes 524288 | tf_op jit(solution)/shard_map/all_to_all | solution.py:44
  27.2 1.7 copy.53
  28.9 0.4 subtract_compare_fusion.2
  29.3 8.9 %all-to-all-done.2 = bf16[32,16,256]{2,0,1:T(8,128)(2,1)S(1)} async-done(((bf16[32,16,256]{2,0,1:T(8,128)(2,1)}), bf16[32,16,256]{2,0,1:T(8,128)(2,1)S(1)}, u32[]{:S(2)}, u32[]{:S(2)}) %all-to-all-start.2) | async-done | bytes 262176 | tf_op jit(solution)/shard_map/all_to_all | solution.py:44
  38.2 3.4 %all-to-all-start.1 = ((bf16[32,16,256]{2,0,1:T(8,128)(2,1)}), bf16[32,16,256]{2,0,1:T(8,128)(2,1)S(1)}, u32[]{:S(2)}, u32[]{:S(2)}) async-start(bf16[32,16,256]{2,0,1:T(8,128)(2,1)} %bitcast.47), calls=%async_computation.1 | async-start | bytes 524288 | tf_op jit(solution)/shard_map/all_to_all | solution.py:42
  41.6 1.3 fusion.7
  42.9 0.1 reshape.152
  43.0 3.7 %collective-permute-start = (bf16[512,2,128]{2,0,1:T(8,128)(2,1)S(1)}, bf16[512,2,128]{2,0,1:T(8,128)(2,1)}, u32[]{:S(2)}, u32[]{:S(2)}) collective-permute-start(bf16[512,2,128]{2,0,1:T(8,128)(2,1)S(1)} %copy.21), channel_id=1, source_target_pairs={{0,32},{16,48},{32,64},{48,80},{64,96},{80,112},{96,128},{112,144}... | collective-permute-start | bytes 786440 | tf_op jit(solution)/shard_map/ppermute | solution.py:15
  46.7 2.9 %collective-permute-start.1 = (bf16[512,2,128]{2,0,1:T(8,128)(2,1)S(1)}, bf16[512,2,128]{2,0,1:T(8,128)(2,1)}, u32[]{:S(2)}, u32[]{:S(2)}) collective-permute-start(bf16[512,2,128]{2,0,1:T(8,128)(2,1)S(1)} %copy.21), channel_id=1, source_target_pairs={{0,16},{16,32},{32,48},{48,64},{64,80},{80,96},{96,112},{112,128},... | collective-permute-start | bytes 786440 | tf_op jit(solution)/shard_map/ppermute | solution.py:15
  49.7 0.1 reshape_reshape.6
  49.7 0.1 reshape_reshape.7
  49.8 0.1 reshape.155
  49.9 4.8 %collective-permute-start.2 = (bf16[512,2,128]{2,0,1:T(8,128)(2,1)S(1)}, bf16[512,2,128]{2,0,1:T(8,128)(2,1)}, u32[]{:S(2)}, u32[]{:S(2)}) collective-permute-start(bf16[512,2,128]{2,0,1:T(8,128)(2,1)S(1)} %copy.29), channel_id=1, source_target_pairs={{0,32},{16,48},{32,64},{48,80},{64,96},{80,112},{96,128},{112,144}... | collective-permute-start | bytes 786440 | tf_op jit(solution)/shard_map/ppermute | solution.py:15
  54.7 3.8 %collective-permute-start.3 = (bf16[512,2,128]{2,0,1:T(8,128)(2,1)S(1)}, bf16[512,2,128]{2,0,1:T(8,128)(2,1)}, u32[]{:S(2)}, u32[]{:S(2)}) collective-permute-start(bf16[512,2,128]{2,0,1:T(8,128)(2,1)S(1)} %copy.29), channel_id=1, source_target_pairs={{0,16},{16,32},{32,48},{48,64},{64,80},{80,96},{96,112},{112,128},... | collective-permute-start | bytes 786440 | tf_op jit(solution)/shard_map/ppermute | solution.py:15
  58.5 0.0 all-to-all-done.1
  58.5 0.1 reshape.153
  58.6 52.4 %all_gather.6 = bf16[1024,2,128]{2,0,1:T(8,128)(2,1)S(1)} all-gather(bf16[32,2,128]{2,0,1:T(8,128)(2,1)S(1)} %bitcast.58), channel_id=1, replica_groups=mesh['ctx'=32,'head'=16] {'ctx'}, dimensions={0}, use_global_device_ids=true | all-gather | bytes 540672 | tf_op jit(solution)/shard_map/all_gather | solution.py:69
  111.1 37.2 %all_gather.7 = bf16[1024,2,128]{2,0,1:T(8,128)(2,1)S(1)} all-gather(bf16[32,2,128]{2,0,1:T(8,128)(2,1)S(1)} %bitcast.59), channel_id=1, replica_groups=mesh['ctx'=32,'head'=16] {'ctx'}, dimensions={0}, use_global_device_ids=true | all-gather | bytes 540672 | tf_op jit(solution)/shard_map/all_gather | solution.py:70
  148.2 1.1 fusion.3
  149.3 0.0 collective-permute-done
  149.3 0.0 collective-permute-done.1
  149.3 2.4 %fusion = (f32[2,512]{1,0:T(2,128)S(1)}, f32[2,1536,512]{2,1,0:T(8,128)S(1)}) fusion(pred[512,1536]{0,1:T(8,128)(4,1)S(1)} %fusion.7, bf16[512,2,128]{2,1,0:T(2,128)(2,1)S(1)} %reshape.153, bf16[512,2,128]{2,0,1:T(8,128)(2,1)S(1)} %copy.21, bf16[512,2,128]{2,0,1:T(8,128)(2,1)} %collective-permute-done.1, bf16[512,2,128]{2,0,1:T(8,128)(2,1)} %collective-permute-done), kind=kOutput, calls=%fused_computation.2 | convolution fusion | flops 409730048 | bytes 8130560 | tf_op jit(solution)/shard_map/qhd,khd->hqk/dot_general | solution.py:24
  151.8 1.7 fusion.1
  153.4 1.6 fusion.11
  155.0 1.5 fusion.9
  156.6 0.0 collective-permute-done.2
  156.6 0.0 collective-permute-done.3
  156.6 3.6 %fusion.23 = bf16[512,2,128]{2,0,1:T(8,128)(2,1)S(1)} fusion(f32[2,512,128]{2,1,0:T(8,128)S(1)} %fusion.11, f32[2,1536,512]{2,1,0:T(8,128)S(1)} %get-tuple-element.6, f32[2,512]{1,0:T(2,128)S(1)} %max.7, pred[512,1536]{0,1:T(8,128)(4,1)S(1)} %fusion.7, bf16[512,2,128]{2,0,1:T(8,128)(2,1)S(1)} %copy.29, bf16[512,2,128]{2,0,1:T(8,128)(2,1)} %collective-permute-done.3, ...), kind=kOutput, calls=%fused_computation.22 | convolution fusion | flops 413270016 | bytes 8658944 | tf_op jit(solution)/shard_map/hqk,khd->hqd/dot_general | solution.py:81
  160.2 0.3 copy.34
  160.4 0.2 all_to_all.59
  160.6 41.6 %all_to_all.67 = bf16[16,32,256]{2,1,0:T(8,128)(2,1)S(1)} all-to-all(bf16[16,32,256]{2,1,0:T(8,128)(2,1)S(1)} %all_to_all.59), channel_id=1, replica_groups=mesh['ctx'=32,'head'=16] {'head'}, dimensions={0} | all-to-all | bytes 524288 | tf_op jit(solution)/shard_map/all_to_all | solution.py:89
  202.2 0.7 copy.40
  (12 shorter events, 0.1 us)
Async XLA Ops:
  1.7 22.1 %all-to-all-start = ((bf16[32,16,256]{2,0,1:T(8,128)(2,1)}), bf16[32,16,256]{2,0,1:T(8,128)(2,1)S(1)}, u32[]{:S(2)}, u32[]{:S(2)}) async-start(bf16[32,16,256]{2,0,1:T(8,128)(2,1)} %bitcast.48), calls=%async_computation | async-start | bytes 524288 | tf_op jit(solution)/shard_map/all_to_all | solution.py:43
  23.7 14.5 %all-to-all-start.2 = ((bf16[32,16,256]{2,0,1:T(8,128)(2,1)}), bf16[32,16,256]{2,0,1:T(8,128)(2,1)S(1)}, u32[]{:S(2)}, u32[]{:S(2)}) async-start(bf16[32,16,256]{2,0,1:T(8,128)(2,1)} %bitcast.46), calls=%async_computation.2 | async-start | bytes 524288 | tf_op jit(solution)/shard_map/all_to_all | solution.py:44
  38.2 20.3 %all-to-all-start.1 = ((bf16[32,16,256]{2,0,1:T(8,128)(2,1)}), bf16[32,16,256]{2,0,1:T(8,128)(2,1)S(1)}, u32[]{:S(2)}, u32[]{:S(2)}) async-start(bf16[32,16,256]{2,0,1:T(8,128)(2,1)} %bitcast.47), calls=%async_computation.1 | async-start | bytes 524288 | tf_op jit(solution)/shard_map/all_to_all | solution.py:42
  43.0 106.3 %collective-permute-start = (bf16[512,2,128]{2,0,1:T(8,128)(2,1)S(1)}, bf16[512,2,128]{2,0,1:T(8,128)(2,1)}, u32[]{:S(2)}, u32[]{:S(2)}) collective-permute-start(bf16[512,2,128]{2,0,1:T(8,128)(2,1)S(1)} %copy.21), channel_id=1, source_target_pairs={{0,32},{16,48},{32,64},{48,80},{64,96},{80,112},{96,128},{112,144}... | collective-permute-start | bytes 786440 | tf_op jit(solution)/shard_map/ppermute | solution.py:15
  46.7 102.6 %collective-permute-start.1 = (bf16[512,2,128]{2,0,1:T(8,128)(2,1)S(1)}, bf16[512,2,128]{2,0,1:T(8,128)(2,1)}, u32[]{:S(2)}, u32[]{:S(2)}) collective-permute-start(bf16[512,2,128]{2,0,1:T(8,128)(2,1)S(1)} %copy.21), channel_id=1, source_target_pairs={{0,16},{16,32},{32,48},{48,64},{64,80},{80,96},{96,112},{112,128},... | collective-permute-start | bytes 786440 | tf_op jit(solution)/shard_map/ppermute | solution.py:15
  49.9 106.6 %collective-permute-start.2 = (bf16[512,2,128]{2,0,1:T(8,128)(2,1)S(1)}, bf16[512,2,128]{2,0,1:T(8,128)(2,1)}, u32[]{:S(2)}, u32[]{:S(2)}) collective-permute-start(bf16[512,2,128]{2,0,1:T(8,128)(2,1)S(1)} %copy.29), channel_id=1, source_target_pairs={{0,32},{16,48},{32,64},{48,80},{64,96},{80,112},{96,128},{112,144}... | collective-permute-start | bytes 786440 | tf_op jit(solution)/shard_map/ppermute | solution.py:15
  54.7 101.9 %collective-permute-start.3 = (bf16[512,2,128]{2,0,1:T(8,128)(2,1)S(1)}, bf16[512,2,128]{2,0,1:T(8,128)(2,1)}, u32[]{:S(2)}, u32[]{:S(2)}) collective-permute-start(bf16[512,2,128]{2,0,1:T(8,128)(2,1)S(1)} %copy.29), channel_id=1, source_target_pairs={{0,16},{16,32},{32,48},{48,64},{64,80},{80,96},{96,112},{112,128},... | collective-permute-start | bytes 786440 | tf_op jit(solution)/shard_map/ppermute | solution.py:15
where the time goes:
time: 204 us; the launch traced here: 203 us
  blocking collectives  131 us (64%)
  starting transfers between devices  32.3 us (16%)
  waiting for transfers between devices  19.1 us (9%)
  matrix products  8.69 us (4%)
  local copies, waits for them, and re-layouts  6.62 us (3%)
  other arithmetic  4.88 us (2%)
    all_gather x1, blocking collectives, local(): lax.all_gather(k_sum, 'ctx', axis=0, tiled=True)  52.4 us
    all_to_all x1, blocking collectives, local(): lax.all_to_all(local_out, 'head', split_axis=0, concat_axis=1, tiled=True)  41.6 us
    all_gather x1, blocking collectives, local(): lax.all_gather(v_sum, 'ctx', axis=0, tiled=True)  37.2 us
    ppermute x4, starting transfers between devices, from_behind(): lax.ppermute(value, axis, [(source, source + steps) for source in range(i...  15.3 us
    all_to_all x1, starting transfers between devices, local(): lax.all_to_all(keys, 'head', split_axis=1, concat_axis=0, tiled=True)  10.2 us
    all_to_all x1, waiting for transfers between devices, local(): lax.all_to_all(keys, 'head', split_axis=1, concat_axis=0, tiled=True)  10.2 us
    all_to_all x1, waiting for transfers between devices, local(): lax.all_to_all(values, 'head', split_axis=1, concat_axis=0, tiled=True)  8.91 us
  transfers between devices with their start and end apart: 7, of which 2 were waited for; matrix products, arithmetic and copies ran while one was open for 7% of the time, Pallas kernels for 0%

commit v1 on v0

--- a/solution.py
+++ b/solution.py
@@ -39,7 +39,12 @@
 
 def local(queries, keys, values):
     q_dev, k_dev, v_dev = (
-        lax.all_to_all(queries, "head", split_axis=1, concat_axis=0, tiled=True),
+        jnp.concatenate(
+            lax.all_to_all(
+                jnp.stack(jnp.split(queries, lax.axis_size("head"), axis=1)), "head", 0, 0
+            ),
+            axis=0,
+        ),
         lax.all_to_all(keys, "head", split_axis=1, concat_axis=0, tiled=True),
         lax.all_to_all(values, "head", split_axis=1, concat_axis=0, tiled=True),
     )

time: 204 us -> 219 us (1.074)
  local copies, waits for them, and re-layouts: 6.62 us -> 26 us
  waiting for transfers between devices: 19.1 us -> 10.7 us
  starting transfers between devices: 32.3 us -> 36.1 us
    unnamed x0 -> x15, local copies, waits for them, and re-layouts: none -> 19.8 us
    all_to_all x1, waiting for transfers between devices: 10.2 us -> 0.01 us  [local(): lax.all_to_all(keys, 'head', split_axis=1, concat_axis=0, tiled=True)]
    all_to_all x1, starting transfers between devices: 3.43 us -> 7.27 us  [local(): lax.all_to_all(values, 'head', split_axis=1, concat_axis=0, tiled=True)]
  transfers between devices with their start and end apart: 7 -> 7, of which waited for: 2 -> 1; matrix products, arithmetic and copies ran while one was open for 7% -> 15% of each run, Pallas kernels for 0% -> 0%
where the time goes in v1:
time: 219 us; the launch traced here: 218 us
  blocking collectives  131 us (60%)
  starting transfers between devices  36.1 us (16%)
  local copies, waits for them, and re-layouts  26 us (12%)
  waiting for transfers between devices  10.7 us (5%)
  matrix products  8.42 us (4%)
  other arithmetic  5.13 us (2%)
    all_gather x1, blocking collectives, local(): lax.all_gather(k_sum, 'ctx', axis=0, tiled=True)  53 us
    all_to_all x1, blocking collectives, local(): lax.all_to_all(local_out, 'head', split_axis=0, concat_axis=1, tiled=True)  41.1 us
    all_gather x1, blocking collectives, local(): lax.all_gather(v_sum, 'ctx', axis=0, tiled=True)  36.8 us
    unnamed x15, local copies, waits for them, and re-layouts  19.8 us
    ppermute x4, starting transfers between devices, from_behind(): lax.ppermute(value, axis, [(source, source + steps) for source in range(i...  15.2 us
    all_to_all x1, waiting for transfers between devices, local(): lax.all_to_all(values, 'head', split_axis=1, concat_axis=0, tiled=True)  10.7 us
    all_to_all x1, starting transfers between devices, local(): lax.all_to_all(keys, 'head', split_axis=1, concat_axis=0, tiled=True)  10.2 us
    all_to_all x1, starting transfers between devices, local(): lax.all_to_all(values, 'head', split_axis=1, concat_axis=0, tiled=True)  7.27 us
  transfers between devices with their start and end apart: 7, of which 1 were waited for; matrix products, arithmetic and copies ran while one was open for 15% of the time, Pallas kernels for 0%

profile of v1, /device:TPU:1, one launch (start us, length us, event | category | flops | bytes accessed | tf_op | source)
XLA Modules:
  0.0 217.5 jit_solution(7318320708700478893)
XLA Ops:
  0.0 1.7 copy.45
  1.7 10.2 %all-to-all-start.1 = ((bf16[32,16,256]{2,0,1:T(8,128)(2,1)}), bf16[32,16,256]{2,0,1:T(8,128)(2,1)S(1)}, u32[]{:S(2)}, u32[]{:S(2)}) async-start(bf16[32,16,256]{2,0,1:T(8,128)(2,1)} %bitcast.56), calls=%async_computation.1 | async-start | bytes 524288 | tf_op jit(solution)/shard_map/all_to_all | solution.py:48
  11.9 1.3 constant_dynamic-update-slice_fusion.15
  13.2 1.3 constant_dynamic-update-slice_fusion.14
  14.5 1.3 constant_dynamic-update-slice_fusion.13
  15.8 1.3 constant_dynamic-update-slice_fusion.12
  17.2 1.3 constant_dynamic-update-slice_fusion.11
  18.5 1.3 constant_dynamic-update-slice_fusion.10
  19.8 1.3 constant_dynamic-update-slice_fusion.9
  21.1 1.3 constant_dynamic-update-slice_fusion.8
  22.4 1.3 constant_dynamic-update-slice_fusion.7
  23.8 1.3 constant_dynamic-update-slice_fusion.6
  25.1 1.3 constant_dynamic-update-slice_fusion.5
  26.4 1.3 constant_dynamic-update-slice_fusion.4
  27.7 1.3 constant_dynamic-update-slice_fusion.3
  29.0 1.3 constant_dynamic-update-slice_fusion.2
  30.4 1.7 copy.44
  32.0 1.3 constant_dynamic-update-slice_fusion.1
  33.4 1.3 constant_dynamic-update-slice_fusion
  34.7 0.0 all-to-all-done.1
  34.7 7.3 %all-to-all-start.2 = ((bf16[32,16,256]{2,0,1:T(8,128)(2,1)}), bf16[32,16,256]{2,0,1:T(8,128)(2,1)S(1)}, u32[]{:S(2)}, u32[]{:S(2)}) async-start(bf16[32,16,256]{2,0,1:T(8,128)(2,1)} %bitcast.55), calls=%async_computation.2 | async-start | bytes 524288 | tf_op jit(solution)/shard_map/all_to_all | solution.py:49
  42.0 1.0 fusion.7
  42.9 10.7 %all-to-all-done.2 = bf16[32,16,256]{2,0,1:T(8,128)(2,1)S(1)} async-done(((bf16[32,16,256]{2,0,1:T(8,128)(2,1)}), bf16[32,16,256]{2,0,1:T(8,128)(2,1)S(1)}, u32[]{:S(2)}, u32[]{:S(2)}) %all-to-all-start.2) | async-done | bytes 262176 | tf_op jit(solution)/shard_map/all_to_all | solution.py:49
  53.7 3.4 %all-to-all-start = ((bf16[16,32,256]{2,1,0:T(8,128)(2,1)}), bf16[16,32,256]{2,1,0:T(8,128)(2,1)S(1)}, u32[]{:S(2)}, u32[]{:S(2)}) async-start(bf16[16,32,256]{2,1,0:T(8,128)(2,1)} %constant_dynamic-update-slice_fusion), calls=%async_computation | async-start | bytes 524288 | tf_op jit(solution)/shard_map/all_to_all | solution.py:43
  57.1 0.4 subtract_compare_fusion.2
  57.5 0.1 reshape.145
  57.6 3.7 %collective-permute-start = (bf16[512,2,128]{2,0,1:T(8,128)(2,1)S(1)}, bf16[512,2,128]{2,0,1:T(8,128)(2,1)}, u32[]{:S(2)}, u32[]{:S(2)}) collective-permute-start(bf16[512,2,128]{2,0,1:T(8,128)(2,1)S(1)} %copy.18), channel_id=1, source_target_pairs={{0,32},{16,48},{32,64},{48,80},{64,96},{80,112},{96,128},{112,144}... | collective-permute-start | bytes 786440 | tf_op jit(solution)/shard_map/ppermute | solution.py:15
  61.4 2.9 %collective-permute-start.1 = (bf16[512,2,128]{2,0,1:T(8,128)(2,1)S(1)}, bf16[512,2,128]{2,0,1:T(8,128)(2,1)}, u32[]{:S(2)}, u32[]{:S(2)}) collective-permute-start(bf16[512,2,128]{2,0,1:T(8,128)(2,1)S(1)} %copy.18), channel_id=1, source_target_pairs={{0,16},{16,32},{32,48},{48,64},{64,80},{80,96},{96,112},{112,128},... | collective-permute-start | bytes 786440 | tf_op jit(solution)/shard_map/ppermute | solution.py:15
  64.3 0.1 reshape_reshape.10
  64.3 0.1 reshape_reshape.11
  64.4 0.1 reshape.147
  64.5 4.8 %collective-permute-start.2 = (bf16[512,2,128]{2,0,1:T(8,128)(2,1)S(1)}, bf16[512,2,128]{2,0,1:T(8,128)(2,1)}, u32[]{:S(2)}, u32[]{:S(2)}) collective-permute-start(bf16[512,2,128]{2,0,1:T(8,128)(2,1)S(1)} %copy.25), channel_id=1, source_target_pairs={{0,32},{16,48},{32,64},{48,80},{64,96},{80,112},{96,128},{112,144}... | collective-permute-start | bytes 786440 | tf_op jit(solution)/shard_map/ppermute | solution.py:15
  69.3 3.8 %collective-permute-start.3 = (bf16[512,2,128]{2,0,1:T(8,128)(2,1)S(1)}, bf16[512,2,128]{2,0,1:T(8,128)(2,1)}, u32[]{:S(2)}, u32[]{:S(2)}) collective-permute-start(bf16[512,2,128]{2,0,1:T(8,128)(2,1)S(1)} %copy.25), channel_id=1, source_target_pairs={{0,16},{16,32},{32,48},{48,64},{64,80},{80,96},{96,112},{112,128},... | collective-permute-start | bytes 786440 | tf_op jit(solution)/shard_map/ppermute | solution.py:15
  73.2 53.0 %all_gather.6 = bf16[1024,2,128]{2,0,1:T(8,128)(2,1)S(1)} all-gather(bf16[32,2,128]{2,0,1:T(8,128)(2,1)S(1)} %bitcast.64), channel_id=1, replica_groups=mesh['ctx'=32,'head'=16] {'ctx'}, dimensions={0}, use_global_device_ids=true | all-gather | bytes 540672 | tf_op jit(solution)/shard_map/all_gather | solution.py:74
  126.2 36.8 %all_gather.7 = bf16[1024,2,128]{2,0,1:T(8,128)(2,1)S(1)} all-gather(bf16[32,2,128]{2,0,1:T(8,128)(2,1)S(1)} %bitcast.65), channel_id=1, replica_groups=mesh['ctx'=32,'head'=16] {'ctx'}, dimensions={0}, use_global_device_ids=true | all-gather | bytes 540672 | tf_op jit(solution)/shard_map/all_gather | solution.py:75
  163.0 0.1 reshape_reshape.9
  163.1 1.1 fusion.3
  164.2 0.0 collective-permute-done.1
  164.2 2.7 %fusion = (f32[2,512]{1,0:T(2,128)S(1)}, f32[2,512,1536]{2,1,0:T(8,128)S(1)}) fusion(pred[512,1536]{1,0:T(8,128)(4,1)S(1)} %fusion.7, bf16[512,2,128]{2,0,1:T(8,128)(2,1)S(1)} %copy.18, bf16[512,2,128]{2,0,1:T(8,128)(2,1)} %collective-permute-done.1, bf16[512,2,128]{2,0,1:T(8,128)(2,1)} %collective-permute-done, bf16[512,2,128]{2,1,0:T(2,128)(2,1)S(1)} %reshape_reshape.9), kind=kOutput, calls=%fused_computation.2 | convolution fusion | flops 409730048 | bytes 8130560 | tf_op jit(solution)/shard_map/qhd,khd->hqk/dot_general | solution.py:24
  166.9 2.2 %fusion.1 = f32[2,512]{1,0:T(2,128)S(1)} fusion(f32[2,512,1536]{2,1,0:T(8,128)S(1)} %get-tuple-element.6, f32[2,512]{1,0:T(2,128)S(1)} %max.7, pred[512,1536]{1,0:T(8,128)(4,1)S(1)} %fusion.7), kind=kLoop, calls=%fused_computation.5 | loop fusion | flops 7863296 | bytes 7086080 | tf_op jit(solution)/shard_map/reduce_sum | solution.py:85
  169.1 1.6 fusion.11
  170.7 1.5 fusion.9
  172.2 0.0 collective-permute-done.2
  172.2 3.1 %fusion.23 = bf16[512,2,128]{2,0,1:T(8,128)(2,1)S(1)} fusion(f32[2,512,128]{2,1,0:T(8,128)S(1)} %fusion.11, f32[2,512,1536]{2,1,0:T(8,128)S(1)} %get-tuple-element.6, f32[2,512]{1,0:T(2,128)S(1)} %max.7, pred[512,1536]{1,0:T(8,128)(4,1)S(1)} %fusion.7, bf16[512,2,128]{2,0,1:T(8,128)(2,1)S(1)} %copy.25, bf16[512,2,128]{2,0,1:T(8,128)(2,1)} %collective-permute-done.3, ...), kind=kOutput, calls=%fused_computation.22 | convolution fusion | flops 413270016 | bytes 8658944 | tf_op jit(solution)/shard_map/hqk,khd->hqd/dot_general | solution.py:86
  175.3 0.3 copy.29
  175.6 0.2 all_to_all.48
  175.8 41.1 %all_to_all.56 = bf16[16,32,256]{2,1,0:T(8,128)(2,1)S(1)} all-to-all(bf16[16,32,256]{2,1,0:T(8,128)(2,1)S(1)} %all_to_all.48), channel_id=1, replica_groups=mesh['ctx'=32,'head'=16] {'head'}, dimensions={0} | all-to-all | bytes 524288 | tf_op jit(solution)/shard_map/all_to_all | solution.py:94
  216.8 0.7 copy.33
  (15 shorter events, 0.2 us)
Async XLA Ops:
  1.7 33.0 %all-to-all-start.1 = ((bf16[32,16,256]{2,0,1:T(8,128)(2,1)}), bf16[32,16,256]{2,0,1:T(8,128)(2,1)S(1)}, u32[]{:S(2)}, u32[]{:S(2)}) async-start(bf16[32,16,256]{2,0,1:T(8,128)(2,1)} %bitcast.56), calls=%async_computation.1 | async-start | bytes 524288 | tf_op jit(solution)/shard_map/all_to_all | solution.py:48
  34.7 19.0 %all-to-all-start.2 = ((bf16[32,16,256]{2,0,1:T(8,128)(2,1)}), bf16[32,16,256]{2,0,1:T(8,128)(2,1)S(1)}, u32[]{:S(2)}, u32[]{:S(2)}) async-start(bf16[32,16,256]{2,0,1:T(8,128)(2,1)} %bitcast.55), calls=%async_computation.2 | async-start | bytes 524288 | tf_op jit(solution)/shard_map/all_to_all | solution.py:49
  53.7 109.4 %all-to-all-start = ((bf16[16,32,256]{2,1,0:T(8,128)(2,1)}), bf16[16,32,256]{2,1,0:T(8,128)(2,1)S(1)}, u32[]{:S(2)}, u32[]{:S(2)}) async-start(bf16[16,32,256]{2,1,0:T(8,128)(2,1)} %constant_dynamic-update-slice_fusion), calls=%async_computation | async-start | bytes 524288 | tf_op jit(solution)/shard_map/all_to_all | solution.py:43
  57.6 106.6 %collective-permute-start = (bf16[512,2,128]{2,0,1:T(8,128)(2,1)S(1)}, bf16[512,2,128]{2,0,1:T(8,128)(2,1)}, u32[]{:S(2)}, u32[]{:S(2)}) collective-permute-start(bf16[512,2,128]{2,0,1:T(8,128)(2,1)S(1)} %copy.18), channel_id=1, source_target_pairs={{0,32},{16,48},{32,64},{48,80},{64,96},{80,112},{96,128},{112,144}... | collective-permute-start | bytes 786440 | tf_op jit(solution)/shard_map/ppermute | solution.py:15
  61.4 102.8 %collective-permute-start.1 = (bf16[512,2,128]{2,0,1:T(8,128)(2,1)S(1)}, bf16[512,2,128]{2,0,1:T(8,128)(2,1)}, u32[]{:S(2)}, u32[]{:S(2)}) collective-permute-start(bf16[512,2,128]{2,0,1:T(8,128)(2,1)S(1)} %copy.18), channel_id=1, source_target_pairs={{0,16},{16,32},{32,48},{48,64},{64,80},{80,96},{96,112},{112,128},... | collective-permute-start | bytes 786440 | tf_op jit(solution)/shard_map/ppermute | solution.py:15
  64.5 107.7 %collective-permute-start.2 = (bf16[512,2,128]{2,0,1:T(8,128)(2,1)S(1)}, bf16[512,2,128]{2,0,1:T(8,128)(2,1)}, u32[]{:S(2)}, u32[]{:S(2)}) collective-permute-start(bf16[512,2,128]{2,0,1:T(8,128)(2,1)S(1)} %copy.25), channel_id=1, source_target_pairs={{0,32},{16,48},{32,64},{48,80},{64,96},{80,112},{96,128},{112,144}... | collective-permute-start | bytes 786440 | tf_op jit(solution)/shard_map/ppermute | solution.py:15
  69.3 102.9 %collective-permute-start.3 = (bf16[512,2,128]{2,0,1:T(8,128)(2,1)S(1)}, bf16[512,2,128]{2,0,1:T(8,128)(2,1)}, u32[]{:S(2)}, u32[]{:S(2)}) collective-permute-start(bf16[512,2,128]{2,0,1:T(8,128)(2,1)S(1)} %copy.25), channel_id=1, source_target_pairs={{0,16},{16,32},{32,48},{48,64},{64,80},{80,96},{96,112},{112,128},... | collective-permute-start | bytes 786440 | tf_op jit(solution)/shard_map/ppermute | solution.py:15
